TPU v7x, 32 devices: a whole 2x2x4 slice. The times are simulated.
32 devices in a mesh: section: 4 (over x, core), obs: 8 (over z, y).
Axes of the slice: x: 2, y: 2, z: 4, core: 2. Of those that a mesh axis runs over, the one named last changes fastest.
Arguments:
- predictors: bfloat16 [4, 4, 20, 32768], P('section', None, None, 'obs'), may hold values from -5 to 5
- departures: float32 [4, 4, 32768], P('section', None, 'obs'), may hold values from -30 to 30
- obs_precision: float32 [4, 4, 32768], P('section', None, 'obs'), may hold values from 0.3 to 3
- qc_pass: int32 [4, 4, 32768], P('section', None, 'obs'), may hold values 0 or 1
- block_channel: int32 [4, 4, 256], P('section', None, 'obs'), may hold values from 0 to 2047, as said below
- stream_order: int32 [4], replicated, may hold values from 0 to 3, each once
- prior_coeffs: float32 [4, 20, 2048], P(None, None, 'obs'), may hold values from -1 to 1
- prior_info: float32 [4, 210, 2048], P(None, None, 'obs'), may hold values from -1 to 32, as said below
- memory_factor: float32 [2048], P('obs'), may hold values from 0.5 to 0.98
Outputs:
- coeffs: float32 [4, 4, 20, 2048], P('section', None, None, 'obs')
- information: float32 [4, 4, 210, 2048], P('section', None, None, 'obs')
Inputs may be any that keep to these rules, and one draw needn't show every extreme that they name: `block_channel`: among the 32 row blocks of one index of obs, at most 8 have channels in any one range of the 256 channels from a multiple of 256; in every window and stream one such range holds exactly 8 blocks of every index of obs. `stream_order`: each stream appears once. `prior_info`: for every stream and channel the 210 entries are the upper triangle, row by row, of a symmetric positive definite matrix of order 20.
All inputs are finite; a program needn't handle non-finite values. No bound on the sum of `qc_pass` on one device may be relied on, other than what follows from the above.
Results may differ from a plain program's by a relative error of at most 0.0038.
Values sent between devices are 32-bit elements; how exact they have to be, the bound alone decides.
A program may use at most 64 MiB of HBM per device.

v0:
```python
import jax
import jax.numpy as jnp
import numpy as np
from jax import lax
from jax.sharding import PartitionSpec as P

HUBER_SQ = 9.0
PRIOR_WEIGHT = 64.0


def from_behind(array, axis, by):
    size = lax.axis_size(axis)
    pairs = [(i, i + by) for i in range(size) if 0 <= i + by < size]
    return lax.ppermute(array, axis, pairs)


def upper_positions(dimension):
    return np.array(
        [i * dimension + j for i in range(dimension) for j in range(i, dimension)], dtype=np.int32
    )


def solve_packed(packed, target):
    dimension = target.shape[0]
    placing = {}
    counter = 0
    for i in range(dimension):
        for j in range(i, dimension):
            placing[i, j] = counter
            counter += 1
    factor = [[None] * dimension for i in range(dimension)]
    for j in range(dimension):
        pivot_root = jnp.sqrt(
            packed[placing[j, j]] - sum((factor[j][k] * factor[j][k] for k in range(j)))
        )
        factor[j][j] = pivot_root
        for i in range(j + 1, dimension):
            factor[i][j] = (
                packed[placing[j, i]] - sum((factor[i][k] * factor[j][k] for k in range(j)))
            ) / pivot_root
    forward = []
    for i in range(dimension):
        forward.append(
            (target[i] - sum((factor[i][k] * forward[k] for k in range(i)))) / factor[i][i]
        )
    backward = [None] * dimension
    for i in reversed(range(dimension)):
        backward[i] = (
            forward[i] - sum((factor[k][i] * backward[k] for k in range(i + 1, dimension)))
        ) / factor[i][i]
    return jnp.stack(backward)


def block_terms(predicted, departed, precision, passed, block_coeffs):
    pred_count, row_count = predicted.shape
    block_count = block_coeffs.shape[1]
    block_width = row_count // block_count
    upper_index = upper_positions(pred_count)
    shaped = predicted.reshape(pred_count, block_count, block_width)
    offset = jnp.sum(shaped.astype(jnp.float32) * block_coeffs[:, :, None], axis=0)
    residual = departed.reshape(block_count, block_width) - offset
    scale_row = precision.reshape(block_count, block_width)
    weight = (
        passed.reshape(block_count, block_width).astype(jnp.float32)
        * scale_row
        / (1.0 + scale_row * residual * residual / HUBER_SQ)
    )
    weighted = (weight[None] * shaped.astype(jnp.float32)).astype(jnp.bfloat16)
    chi_square = jnp.sum(weight * residual * residual)
    passed_count = jnp.sum(passed.astype(jnp.float32))
    gram_full = lax.dot_general(
        weighted, shaped, (((2,), (2,)), ((1,), (1,))), preferred_element_type=jnp.float32
    )
    gram_upper = gram_full.reshape(block_count, pred_count * pred_count)[:, upper_index]
    gradient = jnp.sum(weighted.astype(jnp.float32) * residual[None], axis=2).T
    return (jnp.concatenate([gram_upper, gradient], axis=1), jnp.stack([chi_square, passed_count]))


def local(
    predictors,
    departures,
    obs_precision,
    qc_pass,
    block_channel,
    stream_order,
    prior_coeffs,
    prior_info,
    memory_factor,
):
    section_count = lax.axis_size("section")
    obs_devices = lax.axis_size("obs")
    section_place = lax.axis_index("section")
    stream_count = stream_order.shape[0]
    local_channels = memory_factor.shape[0]
    block_count = block_channel.shape[2]
    pred_count = prior_coeffs.shape[1]
    tri_count = prior_info.shape[1]
    column_count = tri_count + pred_count
    capacity = 2 * block_count // obs_devices
    local_line = jnp.arange(local_channels, dtype=jnp.float32)
    owner_line = jnp.arange(obs_devices, dtype=jnp.int32)
    slot_line = jnp.arange(obs_devices * capacity, dtype=jnp.int32)
    highest = lax.Precision.HIGHEST

    def pack_blocks(block_sums, channel):
        owner_index = channel // local_channels
        inner_channel = channel % local_channels
        owner_hot = (owner_index[:, None] == owner_line[None, :]).astype(jnp.int32)
        ranking = jnp.sum((jnp.cumsum(owner_hot, axis=0) - 1) * owner_hot, axis=1)
        slot_of = owner_index * capacity + ranking
        placing = (slot_of[:, None] == slot_line[None, :]).astype(jnp.float32)
        send_rows = lax.dot_general(
            placing,
            block_sums,
            (((0,), (0,)), ((), ())),
            precision=highest,
            preferred_element_type=jnp.float32,
        ).reshape(obs_devices, capacity, column_count)
        send_channel = (
            lax.dot_general(
                placing,
                (inner_channel + 1).astype(jnp.float32),
                (((0,), (0,)), ((), ())),
                precision=highest,
                preferred_element_type=jnp.float32,
            ).reshape(obs_devices, capacity)
            - 1.0
        )
        return (send_rows, send_channel)

    def unpack_blocks(got_rows, got_channel):
        gather_hot = (got_channel.reshape(-1)[:, None] == local_line[None, :]).astype(jnp.float32)
        return lax.dot_general(
            got_rows.reshape(-1, column_count),
            gather_hot,
            (((0,), (0,)), ((), ())),
            precision=highest,
            preferred_element_type=jnp.float32,
        )

    def window_work(state_now, streams):
        beta_prior = state_now[:, :pred_count]
        info_prior = state_now[:, pred_count:]
        all_coeffs = lax.all_gather(beta_prior, "obs", axis=2, tiled=True)
        channel = jnp.take(block_channel[0], streams, axis=0)
        block_coeffs = jax.vmap(lambda coeff_rows, chan: jnp.take(coeff_rows, chan, axis=1))(
            all_coeffs, channel
        )
        block_sums, statistics = jax.vmap(block_terms)(
            jnp.take(predictors[0], streams, axis=0),
            jnp.take(departures[0], streams, axis=0),
            jnp.take(obs_precision[0], streams, axis=0),
            jnp.take(qc_pass[0], streams, axis=0),
            block_coeffs,
        )
        totals = lax.psum(statistics, "obs")
        send_rows, send_channel = jax.vmap(pack_blocks)(block_sums, channel)
        got_rows, got_channel = (
            lax.all_to_all(send_rows, "obs", split_axis=1, concat_axis=1, tiled=True),
            lax.all_to_all(send_channel, "obs", split_axis=1, concat_axis=1, tiled=True),
        )
        normal = jax.vmap(unpack_blocks)(got_rows, got_channel)
        inflation = (totals[:, 0] + PRIOR_WEIGHT) / (totals[:, 1] + PRIOR_WEIGHT)
        info_post = info_prior + normal[:, :tri_count] / inflation[:, None, None]
        beta_post = beta_prior + jax.vmap(solve_packed)(
            info_post, normal[:, tri_count:] / inflation[:, None, None]
        )
        outgoing = jnp.concatenate([beta_post, memory_factor[None, None, :] * info_post], axis=1)
        incoming = from_behind(outgoing, "section", 1)
        return (beta_post, info_post, incoming)

    def fresh_of(streams):
        return jnp.concatenate(
            [jnp.take(prior_coeffs, streams, axis=0), jnp.take(prior_info, streams, axis=0)], axis=1
        )

    coeff_start = jnp.zeros((1, stream_count, pred_count, local_channels), jnp.float32)
    info_start = jnp.zeros((1, stream_count, tri_count, local_channels), jnp.float32)

    def tick_step(t, loop_state):
        incoming, coeff_out, info_out = loop_state
        entry_index = t - section_place
        usable = (entry_index >= 0) & (entry_index < stream_count)
        slot_index = jnp.clip(entry_index, 0, stream_count - 1)
        streams = lax.dynamic_slice_in_dim(stream_order, slot_index, 1, 0)
        state_now = jnp.where(
            (section_place == 0) | jnp.logical_not(usable), fresh_of(streams), incoming
        )
        beta_post, info_post, incoming = window_work(state_now, streams)

        def store_entry(buffer, result):
            current = lax.dynamic_slice_in_dim(buffer, slot_index, 1, 1)
            updated = jnp.where(usable, result[None], current)
            return lax.dynamic_update_slice_in_dim(buffer, updated, slot_index, 1)

        return (incoming, store_entry(coeff_out, beta_post), store_entry(info_out, info_post))

    initial = (jnp.zeros((1, column_count, local_channels), jnp.float32), coeff_start, info_start)
    final_state = lax.fori_loop(0, stream_count + section_count - 1, tick_step, initial)
    return (final_state[1], final_state[2])


def solution(mesh):
    in_specs = (
        P("section", None, None, "obs"),
        P("section", None, "obs"),
        P("section", None, "obs"),
        P("section", None, "obs"),
        P("section", None, "obs"),
        P(),
        P(None, None, "obs"),
        P(None, None, "obs"),
        P("obs"),
    )
    out_specs = (P("section", None, None, "obs"), P("section", None, None, "obs"))
    return jax.shard_map(local, mesh=mesh, in_specs=in_specs, out_specs=out_specs, check_vma=False)
```

profile of v0, /device:TPU:1, one launch (start us, length us, event | category | flops | bytes accessed | tf_op | source)
XLA Modules:
  0.0 688.5 jit_solution(5905409147109336993)
XLA Ops:
  2.9 684.6 %while.38 = (s32[]{:T(128)}, f32[1,230,256]{2,1,0:T(8,128)S(1)}, f32[1,4,20,256]{3,1,2,0:T(4,128)S(1)}, f32[1,4,210,256]{3,1,2,0:T(4,128)S(1)}, s32[]{:T(128)}, ...) while((s32[]{:T(128)}, f32[1,230,256]{2,1,0:T(8,128)S(1)}, ...), condition=%wide.region_8.10_spmd.clone.clone, body=%wide.region_0.9_spmd.sunk.clone.clone.sunk | while | flops 57759508 | bytes 13853709 | solution.py:199
  7.5 6.4 all-to-all-start.1
  16.3 24.6 %all_gather.15 = f32[1,20,2048]{2,1,0:T(8,128)S(1)} all-gather(f32[1,20,256]{2,1,0:T(8,128)S(1)} %slice.5342), channel_id=1, replica_groups=mesh['section'=4,'obs'=8] {'obs'}, dimensions={2}, use_global_device_ids=true | all-gather | bytes 184320 | tf_op jit(solution)/shard_map/while/body/eval_jaxpr/all_gather | solution.py:144
  47.6 17.5 %psum.19 = f32[1,2]{1,0:T(1,128)S(1)} all-reduce(f32[1,2]{1,0:T(1,128)S(1)} %maximum_bitcast_fusion.6), channel_id=1, replica_groups=mesh['section'=4,'obs'=8] {'obs'}, use_global_device_ids=true, to_apply=%region_7.8 | all-reduce | flops 2 | bytes 16 | tf_op jit(solution)/shard_map/while/body/eval_jaxpr/psum | solution.py:156
  83.2 15.7 %collective-permute-start = (f32[1,230,256]{2,1,0:T(8,128)S(1)}, f32[1,230,256]{2,1,0:T(8,128)S(1)}, u32[]{:S(2)}, u32[]{:S(2)}) collective-permute-start(f32[1,230,256]{2,1,0:T(8,128)S(1)} %pad_maximum_fusion.2), channel_id=1, source_target_pairs={{0,8},{8,16},{16,24},{1,9},{9,17},{17,25},{2,10},{10,18},{18,26},{... | collective-permute-start | bytes 706568 | tf_op jit(solution)/shard_map/while/body/eval_jaxpr/ppermute | solution.py:14
  115.6 25.2 %all_gather.15 = f32[1,20,2048]{2,1,0:T(8,128)S(1)} all-gather(f32[1,20,256]{2,1,0:T(8,128)S(1)} %slice.5342), channel_id=1, replica_groups=mesh['section'=4,'obs'=8] {'obs'}, dimensions={2}, use_global_device_ids=true | all-gather | bytes 184320 | tf_op jit(solution)/shard_map/while/body/eval_jaxpr/all_gather | solution.py:144
  147.5 17.3 %psum.19 = f32[1,2]{1,0:T(1,128)S(1)} all-reduce(f32[1,2]{1,0:T(1,128)S(1)} %maximum_bitcast_fusion.6), channel_id=1, replica_groups=mesh['section'=4,'obs'=8] {'obs'}, use_global_device_ids=true, to_apply=%region_7.8 | all-reduce | flops 2 | bytes 16 | tf_op jit(solution)/shard_map/while/body/eval_jaxpr/psum | solution.py:156
  182.9 13.1 %collective-permute-start = (f32[1,230,256]{2,1,0:T(8,128)S(1)}, f32[1,230,256]{2,1,0:T(8,128)S(1)}, u32[]{:S(2)}, u32[]{:S(2)}) collective-permute-start(f32[1,230,256]{2,1,0:T(8,128)S(1)} %pad_maximum_fusion.2), channel_id=1, source_target_pairs={{0,8},{8,16},{16,24},{1,9},{9,17},{17,25},{2,10},{10,18},{18,26},{... | collective-permute-start | bytes 706568 | tf_op jit(solution)/shard_map/while/body/eval_jaxpr/ppermute | solution.py:14
  212.6 24.6 %all_gather.15 = f32[1,20,2048]{2,1,0:T(8,128)S(1)} all-gather(f32[1,20,256]{2,1,0:T(8,128)S(1)} %slice.5342), channel_id=1, replica_groups=mesh['section'=4,'obs'=8] {'obs'}, dimensions={2}, use_global_device_ids=true | all-gather | bytes 184320 | tf_op jit(solution)/shard_map/while/body/eval_jaxpr/all_gather | solution.py:144
  244.0 17.5 %psum.19 = f32[1,2]{1,0:T(1,128)S(1)} all-reduce(f32[1,2]{1,0:T(1,128)S(1)} %maximum_bitcast_fusion.6), channel_id=1, replica_groups=mesh['section'=4,'obs'=8] {'obs'}, use_global_device_ids=true, to_apply=%region_7.8 | all-reduce | flops 2 | bytes 16 | tf_op jit(solution)/shard_map/while/body/eval_jaxpr/psum | solution.py:156
  279.6 13.4 %collective-permute-start = (f32[1,230,256]{2,1,0:T(8,128)S(1)}, f32[1,230,256]{2,1,0:T(8,128)S(1)}, u32[]{:S(2)}, u32[]{:S(2)}) collective-permute-start(f32[1,230,256]{2,1,0:T(8,128)S(1)} %pad_maximum_fusion.2), channel_id=1, source_target_pairs={{0,8},{8,16},{16,24},{1,9},{9,17},{17,25},{2,10},{10,18},{18,26},{... | collective-permute-start | bytes 706568 | tf_op jit(solution)/shard_map/while/body/eval_jaxpr/ppermute | solution.py:14
  309.7 24.8 %all_gather.15 = f32[1,20,2048]{2,1,0:T(8,128)S(1)} all-gather(f32[1,20,256]{2,1,0:T(8,128)S(1)} %slice.5342), channel_id=1, replica_groups=mesh['section'=4,'obs'=8] {'obs'}, dimensions={2}, use_global_device_ids=true | all-gather | bytes 184320 | tf_op jit(solution)/shard_map/while/body/eval_jaxpr/all_gather | solution.py:144
  341.3 17.6 %psum.19 = f32[1,2]{1,0:T(1,128)S(1)} all-reduce(f32[1,2]{1,0:T(1,128)S(1)} %maximum_bitcast_fusion.6), channel_id=1, replica_groups=mesh['section'=4,'obs'=8] {'obs'}, use_global_device_ids=true, to_apply=%region_7.8 | all-reduce | flops 2 | bytes 16 | tf_op jit(solution)/shard_map/while/body/eval_jaxpr/psum | solution.py:156
  377.0 13.1 %collective-permute-start = (f32[1,230,256]{2,1,0:T(8,128)S(1)}, f32[1,230,256]{2,1,0:T(8,128)S(1)}, u32[]{:S(2)}, u32[]{:S(2)}) collective-permute-start(f32[1,230,256]{2,1,0:T(8,128)S(1)} %pad_maximum_fusion.2), channel_id=1, source_target_pairs={{0,8},{8,16},{16,24},{1,9},{9,17},{17,25},{2,10},{10,18},{18,26},{... | collective-permute-start | bytes 706568 | tf_op jit(solution)/shard_map/while/body/eval_jaxpr/ppermute | solution.py:14
  406.7 24.9 %all_gather.15 = f32[1,20,2048]{2,1,0:T(8,128)S(1)} all-gather(f32[1,20,256]{2,1,0:T(8,128)S(1)} %slice.5342), channel_id=1, replica_groups=mesh['section'=4,'obs'=8] {'obs'}, dimensions={2}, use_global_device_ids=true | all-gather | bytes 184320 | tf_op jit(solution)/shard_map/while/body/eval_jaxpr/all_gather | solution.py:144
  438.4 17.2 %psum.19 = f32[1,2]{1,0:T(1,128)S(1)} all-reduce(f32[1,2]{1,0:T(1,128)S(1)} %maximum_bitcast_fusion.6), channel_id=1, replica_groups=mesh['section'=4,'obs'=8] {'obs'}, use_global_device_ids=true, to_apply=%region_7.8 | all-reduce | flops 2 | bytes 16 | tf_op jit(solution)/shard_map/while/body/eval_jaxpr/psum | solution.py:156
  473.8 13.4 %collective-permute-start = (f32[1,230,256]{2,1,0:T(8,128)S(1)}, f32[1,230,256]{2,1,0:T(8,128)S(1)}, u32[]{:S(2)}, u32[]{:S(2)}) collective-permute-start(f32[1,230,256]{2,1,0:T(8,128)S(1)} %pad_maximum_fusion.2), channel_id=1, source_target_pairs={{0,8},{8,16},{16,24},{1,9},{9,17},{17,25},{2,10},{10,18},{18,26},{... | collective-permute-start | bytes 706568 | tf_op jit(solution)/shard_map/while/body/eval_jaxpr/ppermute | solution.py:14
  487.5 5.9 dynamic_update_slice.31
  503.8 24.8 %all_gather.15 = f32[1,20,2048]{2,1,0:T(8,128)S(1)} all-gather(f32[1,20,256]{2,1,0:T(8,128)S(1)} %slice.5342), channel_id=1, replica_groups=mesh['section'=4,'obs'=8] {'obs'}, dimensions={2}, use_global_device_ids=true | all-gather | bytes 184320 | tf_op jit(solution)/shard_map/while/body/eval_jaxpr/all_gather | solution.py:144
  535.4 17.5 %psum.19 = f32[1,2]{1,0:T(1,128)S(1)} all-reduce(f32[1,2]{1,0:T(1,128)S(1)} %maximum_bitcast_fusion.6), channel_id=1, replica_groups=mesh['section'=4,'obs'=8] {'obs'}, use_global_device_ids=true, to_apply=%region_7.8 | all-reduce | flops 2 | bytes 16 | tf_op jit(solution)/shard_map/while/body/eval_jaxpr/psum | solution.py:156
  571.0 13.2 %collective-permute-start = (f32[1,230,256]{2,1,0:T(8,128)S(1)}, f32[1,230,256]{2,1,0:T(8,128)S(1)}, u32[]{:S(2)}, u32[]{:S(2)}) collective-permute-start(f32[1,230,256]{2,1,0:T(8,128)S(1)} %pad_maximum_fusion.2), channel_id=1, source_target_pairs={{0,8},{8,16},{16,24},{1,9},{9,17},{17,25},{2,10},{10,18},{18,26},{... | collective-permute-start | bytes 706568 | tf_op jit(solution)/shard_map/while/body/eval_jaxpr/ppermute | solution.py:14
  600.9 24.5 %all_gather.15 = f32[1,20,2048]{2,1,0:T(8,128)S(1)} all-gather(f32[1,20,256]{2,1,0:T(8,128)S(1)} %slice.5342), channel_id=1, replica_groups=mesh['section'=4,'obs'=8] {'obs'}, dimensions={2}, use_global_device_ids=true | all-gather | bytes 184320 | tf_op jit(solution)/shard_map/while/body/eval_jaxpr/all_gather | solution.py:144
  632.1 18.0 %psum.19 = f32[1,2]{1,0:T(1,128)S(1)} all-reduce(f32[1,2]{1,0:T(1,128)S(1)} %maximum_bitcast_fusion.6), channel_id=1, replica_groups=mesh['section'=4,'obs'=8] {'obs'}, use_global_device_ids=true, to_apply=%region_7.8 | all-reduce | flops 2 | bytes 16 | tf_op jit(solution)/shard_map/while/body/eval_jaxpr/psum | solution.py:156
  668.2 13.1 %collective-permute-start = (f32[1,230,256]{2,1,0:T(8,128)S(1)}, f32[1,230,256]{2,1,0:T(8,128)S(1)}, u32[]{:S(2)}, u32[]{:S(2)}) collective-permute-start(f32[1,230,256]{2,1,0:T(8,128)S(1)} %pad_maximum_fusion.2), channel_id=1, source_target_pairs={{0,8},{8,16},{16,24},{1,9},{9,17},{17,25},{2,10},{10,18},{18,26},{... | collective-permute-start | bytes 706568 | tf_op jit(solution)/shard_map/while/body/eval_jaxpr/ppermute | solution.py:14
  (656 shorter events, 258.7 us)
Async XLA Ops:
  7.5 60.4 %all-to-all-start.1 = ((f32[1,8,8]{2,0,1:T(1,128)}), f32[1,8,8]{2,0,1:T(1,128)S(1)}, u32[]{:S(2)}, u32[]{:S(2)}) async-start(f32[1,8,8]{2,0,1:T(1,128)} %bitcast.2454), calls=%async_computation.1 | async-start | bytes 8192 | tf_op jit(solution)/shard_map/while/body/eval_jaxpr/all_to_all | solution.py:160
  68.0 9.1 %all-to-all-start = ((f32[1,8,8,230]{3,2,0,1:T(8,128)}), f32[1,8,8,230]{3,2,0,1:T(8,128)S(1)}, u32[]{:S(2)}, u32[]{:S(2)}) async-start(f32[1,8,8,230]{3,2,0,1:T(8,128)} %convolution_bitcast_fusion.4), calls=%async_computation | async-start | bytes 131072 | tf_op jit(solution)/shard_map/while/body/eval_jaxpr/all_to_all | solution.py:159
  83.2 22.0 %collective-permute-start = (f32[1,230,256]{2,1,0:T(8,128)S(1)}, f32[1,230,256]{2,1,0:T(8,128)S(1)}, u32[]{:S(2)}, u32[]{:S(2)}) collective-permute-start(f32[1,230,256]{2,1,0:T(8,128)S(1)} %pad_maximum_fusion.2), channel_id=1, source_target_pairs={{0,8},{8,16},{16,24},{1,9},{9,17},{17,25},{2,10},{10,18},{18,26},{... | collective-permute-start | bytes 706568 | tf_op jit(solution)/shard_map/while/body/eval_jaxpr/ppermute | solution.py:14
  109.8 57.8 %all-to-all-start.1 = ((f32[1,8,8]{2,0,1:T(1,128)}), f32[1,8,8]{2,0,1:T(1,128)S(1)}, u32[]{:S(2)}, u32[]{:S(2)}) async-start(f32[1,8,8]{2,0,1:T(1,128)} %bitcast.2454), calls=%async_computation.1 | async-start | bytes 8192 | tf_op jit(solution)/shard_map/while/body/eval_jaxpr/all_to_all | solution.py:160
  167.6 9.1 %all-to-all-start = ((f32[1,8,8,230]{3,2,0,1:T(8,128)}), f32[1,8,8,230]{3,2,0,1:T(8,128)S(1)}, u32[]{:S(2)}, u32[]{:S(2)}) async-start(f32[1,8,8,230]{3,2,0,1:T(8,128)} %convolution_bitcast_fusion.4), calls=%async_computation | async-start | bytes 131072 | tf_op jit(solution)/shard_map/while/body/eval_jaxpr/all_to_all | solution.py:159
  182.9 19.4 %collective-permute-start = (f32[1,230,256]{2,1,0:T(8,128)S(1)}, f32[1,230,256]{2,1,0:T(8,128)S(1)}, u32[]{:S(2)}, u32[]{:S(2)}) collective-permute-start(f32[1,230,256]{2,1,0:T(8,128)S(1)} %pad_maximum_fusion.2), channel_id=1, source_target_pairs={{0,8},{8,16},{16,24},{1,9},{9,17},{17,25},{2,10},{10,18},{18,26},{... | collective-permute-start | bytes 706568 | tf_op jit(solution)/shard_map/while/body/eval_jaxpr/ppermute | solution.py:14
  206.9 57.5 %all-to-all-start.1 = ((f32[1,8,8]{2,0,1:T(1,128)}), f32[1,8,8]{2,0,1:T(1,128)S(1)}, u32[]{:S(2)}, u32[]{:S(2)}) async-start(f32[1,8,8]{2,0,1:T(1,128)} %bitcast.2454), calls=%async_computation.1 | async-start | bytes 8192 | tf_op jit(solution)/shard_map/while/body/eval_jaxpr/all_to_all | solution.py:160
  264.4 9.1 %all-to-all-start = ((f32[1,8,8,230]{3,2,0,1:T(8,128)}), f32[1,8,8,230]{3,2,0,1:T(8,128)S(1)}, u32[]{:S(2)}, u32[]{:S(2)}) async-start(f32[1,8,8,230]{3,2,0,1:T(8,128)} %convolution_bitcast_fusion.4), calls=%async_computation | async-start | bytes 131072 | tf_op jit(solution)/shard_map/while/body/eval_jaxpr/all_to_all | solution.py:159
  277.1 0.7 copy-start.1
  279.6 19.7 %collective-permute-start = (f32[1,230,256]{2,1,0:T(8,128)S(1)}, f32[1,230,256]{2,1,0:T(8,128)S(1)}, u32[]{:S(2)}, u32[]{:S(2)}) collective-permute-start(f32[1,230,256]{2,1,0:T(8,128)S(1)} %pad_maximum_fusion.2), channel_id=1, source_target_pairs={{0,8},{8,16},{16,24},{1,9},{9,17},{17,25},{2,10},{10,18},{18,26},{... | collective-permute-start | bytes 706568 | tf_op jit(solution)/shard_map/while/body/eval_jaxpr/ppermute | solution.py:14
  303.9 57.8 %all-to-all-start.1 = ((f32[1,8,8]{2,0,1:T(1,128)}), f32[1,8,8]{2,0,1:T(1,128)S(1)}, u32[]{:S(2)}, u32[]{:S(2)}) async-start(f32[1,8,8]{2,0,1:T(1,128)} %bitcast.2454), calls=%async_computation.1 | async-start | bytes 8192 | tf_op jit(solution)/shard_map/while/body/eval_jaxpr/all_to_all | solution.py:160
  361.8 9.1 %all-to-all-start = ((f32[1,8,8,230]{3,2,0,1:T(8,128)}), f32[1,8,8,230]{3,2,0,1:T(8,128)S(1)}, u32[]{:S(2)}, u32[]{:S(2)}) async-start(f32[1,8,8,230]{3,2,0,1:T(8,128)} %convolution_bitcast_fusion.4), calls=%async_computation | async-start | bytes 131072 | tf_op jit(solution)/shard_map/while/body/eval_jaxpr/all_to_all | solution.py:159
  377.0 19.4 %collective-permute-start = (f32[1,230,256]{2,1,0:T(8,128)S(1)}, f32[1,230,256]{2,1,0:T(8,128)S(1)}, u32[]{:S(2)}, u32[]{:S(2)}) collective-permute-start(f32[1,230,256]{2,1,0:T(8,128)S(1)} %pad_maximum_fusion.2), channel_id=1, source_target_pairs={{0,8},{8,16},{16,24},{1,9},{9,17},{17,25},{2,10},{10,18},{18,26},{... | collective-permute-start | bytes 706568 | tf_op jit(solution)/shard_map/while/body/eval_jaxpr/ppermute | solution.py:14
  401.0 57.5 %all-to-all-start.1 = ((f32[1,8,8]{2,0,1:T(1,128)}), f32[1,8,8]{2,0,1:T(1,128)S(1)}, u32[]{:S(2)}, u32[]{:S(2)}) async-start(f32[1,8,8]{2,0,1:T(1,128)} %bitcast.2454), calls=%async_computation.1 | async-start | bytes 8192 | tf_op jit(solution)/shard_map/while/body/eval_jaxpr/all_to_all | solution.py:160
  458.5 9.1 %all-to-all-start = ((f32[1,8,8,230]{3,2,0,1:T(8,128)}), f32[1,8,8,230]{3,2,0,1:T(8,128)S(1)}, u32[]{:S(2)}, u32[]{:S(2)}) async-start(f32[1,8,8,230]{3,2,0,1:T(8,128)} %convolution_bitcast_fusion.4), calls=%async_computation | async-start | bytes 131072 | tf_op jit(solution)/shard_map/while/body/eval_jaxpr/all_to_all | solution.py:159
  473.8 19.7 %collective-permute-start = (f32[1,230,256]{2,1,0:T(8,128)S(1)}, f32[1,230,256]{2,1,0:T(8,128)S(1)}, u32[]{:S(2)}, u32[]{:S(2)}) collective-permute-start(f32[1,230,256]{2,1,0:T(8,128)S(1)} %pad_maximum_fusion.2), channel_id=1, source_target_pairs={{0,8},{8,16},{16,24},{1,9},{9,17},{17,25},{2,10},{10,18},{18,26},{... | collective-permute-start | bytes 706568 | tf_op jit(solution)/shard_map/while/body/eval_jaxpr/ppermute | solution.py:14
  498.1 57.7 %all-to-all-start.1 = ((f32[1,8,8]{2,0,1:T(1,128)}), f32[1,8,8]{2,0,1:T(1,128)S(1)}, u32[]{:S(2)}, u32[]{:S(2)}) async-start(f32[1,8,8]{2,0,1:T(1,128)} %bitcast.2454), calls=%async_computation.1 | async-start | bytes 8192 | tf_op jit(solution)/shard_map/while/body/eval_jaxpr/all_to_all | solution.py:160
  555.8 9.1 %all-to-all-start = ((f32[1,8,8,230]{3,2,0,1:T(8,128)}), f32[1,8,8,230]{3,2,0,1:T(8,128)S(1)}, u32[]{:S(2)}, u32[]{:S(2)}) async-start(f32[1,8,8,230]{3,2,0,1:T(8,128)} %convolution_bitcast_fusion.4), calls=%async_computation | async-start | bytes 131072 | tf_op jit(solution)/shard_map/while/body/eval_jaxpr/all_to_all | solution.py:159
  571.0 19.5 %collective-permute-start = (f32[1,230,256]{2,1,0:T(8,128)S(1)}, f32[1,230,256]{2,1,0:T(8,128)S(1)}, u32[]{:S(2)}, u32[]{:S(2)}) collective-permute-start(f32[1,230,256]{2,1,0:T(8,128)S(1)} %pad_maximum_fusion.2), channel_id=1, source_target_pairs={{0,8},{8,16},{16,24},{1,9},{9,17},{17,25},{2,10},{10,18},{18,26},{... | collective-permute-start | bytes 706568 | tf_op jit(solution)/shard_map/while/body/eval_jaxpr/ppermute | solution.py:14
  595.1 57.8 %all-to-all-start.1 = ((f32[1,8,8]{2,0,1:T(1,128)}), f32[1,8,8]{2,0,1:T(1,128)S(1)}, u32[]{:S(2)}, u32[]{:S(2)}) async-start(f32[1,8,8]{2,0,1:T(1,128)} %bitcast.2454), calls=%async_computation.1 | async-start | bytes 8192 | tf_op jit(solution)/shard_map/while/body/eval_jaxpr/all_to_all | solution.py:160
  652.9 9.1 %all-to-all-start = ((f32[1,8,8,230]{3,2,0,1:T(8,128)}), f32[1,8,8,230]{3,2,0,1:T(8,128)S(1)}, u32[]{:S(2)}, u32[]{:S(2)}) async-start(f32[1,8,8,230]{3,2,0,1:T(8,128)} %convolution_bitcast_fusion.4), calls=%async_computation | async-start | bytes 131072 | tf_op jit(solution)/shard_map/while/body/eval_jaxpr/all_to_all | solution.py:159
  668.2 19.4 %collective-permute-start = (f32[1,230,256]{2,1,0:T(8,128)S(1)}, f32[1,230,256]{2,1,0:T(8,128)S(1)}, u32[]{:S(2)}, u32[]{:S(2)}) collective-permute-start(f32[1,230,256]{2,1,0:T(8,128)S(1)} %pad_maximum_fusion.2), channel_id=1, source_target_pairs={{0,8},{8,16},{16,24},{1,9},{9,17},{17,25},{2,10},{10,18},{18,26},{... | collective-permute-start | bytes 706568 | tf_op jit(solution)/shard_map/while/body/eval_jaxpr/ppermute | solution.py:14
  687.6 0.9 copy-start.2
  687.6 0.9 copy-start.3
  (23 other events, 15.4 us)
where the time goes:
time: 692 us; the launch traced here: 689 us
  blocking collectives  296 us (43%)
  starting transfers between devices  145 us (21%)
  local copies, waits for them, and re-layouts  109 us (16%)
  other arithmetic  68.2 us (10%)
  waiting for transfers between devices  30.8 us (4%)
  loops' own time  25.7 us (4%)
  matrix products  12.9 us (2%)
    all_gather x7, blocking collectives, window_work(): all_coeffs = lax.all_gather(beta_prior, 'obs', axis=2, tiled=True)  173 us
    psum x7, blocking collectives, window_work(): totals = lax.psum(statistics, 'obs')  123 us
    ppermute x7, starting transfers between devices, from_behind(): return lax.ppermute(array, axis, pairs)  95 us
    dynamic_update_slice x28, local copies, waits for them, and re-layouts, store_entry(): return lax.dynamic_update_slice_in_dim(buffer, updated, slot_index, 1)  43.8 us
    all_to_all x7, waiting for transfers between devices, window_work(): lax.all_to_all(send_rows, 'obs', split_axis=1, concat_axis=1, tiled=True)  30.8 us
    all_to_all x7, starting transfers between devices, window_work(): lax.all_to_all(send_channel, 'obs', split_axis=1, concat_axis=1, tiled=True)  26.2 us
    another operation x1, loops' own time, local(): lax.fori_loop(0, stream_count + section_count - 1, tick_step, initial)  25.7 us
    all_to_all x7, starting transfers between devices, window_work(): lax.all_to_all(send_rows, 'obs', split_axis=1, concat_axis=1, tiled=True)  23.5 us
  transfers between devices with their start and end apart: 21, of which 7 were waited for; matrix products, arithmetic and copies ran while one was open for 18% of the time, Pallas kernels for 0%

commit v1 on v0

--- a/solution.py
+++ b/solution.py
@@ -6,6 +6,14 @@
 
 HUBER_SQ = 9.0
 PRIOR_WEIGHT = 64.0
+
+
+def obtain_the_column(patch, which_axis):
+    parts_n = lax.axis_size(which_axis)
+    now = patch
+    for rr in [dd for dd in (1, 2, 4, 8, 16) if dd < parts_n]:
+        now = now + lax.ppermute(now, which_axis, [(p, p ^ rr) for p in range(parts_n)])
+    return now
 
 
 def from_behind(array, axis, by):
@@ -153,7 +161,7 @@
             jnp.take(qc_pass[0], streams, axis=0),
             block_coeffs,
         )
-        totals = lax.psum(statistics, "obs")
+        totals = obtain_the_column(statistics, "obs")
         send_rows, send_channel = jax.vmap(pack_blocks)(block_sums, channel)
         got_rows, got_channel = (
             lax.all_to_all(send_rows, "obs", split_axis=1, concat_axis=1, tiled=True),

time: 692 us -> 626 us (0.905)
  blocking collectives: 296 us -> 174 us
  starting transfers between devices: 145 us -> 167 us
  other arithmetic: 68.2 us -> 86.9 us
  waiting for transfers between devices: 30.8 us -> 46.8 us
    psum x7 -> x0, blocking collectives: 123 us -> none  [window_work(): totals = lax.psum(statistics, 'obs')]
    ppermute x0 -> x21, waiting for transfers between devices: none -> 27.8 us  [obtain_the_column(): lax.ppermute(now, which_axis, [(p, p ^ rr) for p in range(parts_n)])]
    ppermute x0 -> x21, starting transfers between devices: none -> 21 us  [obtain_the_column(): lax.ppermute(now, which_axis, [(p, p ^ rr) for p in range(parts_n)])]
    add x0 -> x21, other arithmetic: none -> 18.5 us  [obtain_the_column(): now + lax.ppermute(now, which_axis, [(p, p ^ rr) for p in range(parts_n)])]
    all_to_all x7, waiting for transfers between devices: 30.8 us -> 19 us  [window_work(): lax.all_to_all(send_rows, 'obs', split_axis=1, concat_axis=1, tiled=True)]
  transfers between devices with their start and end apart: 21 -> 42, of which waited for: 7 -> 21; matrix products, arithmetic and copies ran while one was open for 18% -> 23% of each run, Pallas kernels for 0% -> 0%
where the time goes in v1:
time: 626 us; the launch traced here: 623 us
  blocking collectives  174 us (28%)
  starting transfers between devices  167 us (27%)
  local copies, waits for them, and re-layouts  109 us (17%)
  other arithmetic  86.9 us (14%)
  waiting for transfers between devices  46.8 us (7%)
  loops' own time  26 us (4%)
  matrix products  12.9 us (2%)
    all_gather x7, blocking collectives, window_work(): all_coeffs = lax.all_gather(beta_prior, 'obs', axis=2, tiled=True)  174 us
    ppermute x7, starting transfers between devices, from_behind(): return lax.ppermute(array, axis, pairs)  89.8 us
    dynamic_update_slice x28, local copies, waits for them, and re-layouts, store_entry(): return lax.dynamic_update_slice_in_dim(buffer, updated, slot_index, 1)  43.8 us
    all_to_all x7, starting transfers between devices, window_work(): lax.all_to_all(send_rows, 'obs', split_axis=1, concat_axis=1, tiled=True)  29.5 us
    ppermute x21, waiting for transfers between devices, obtain_the_column(): lax.ppermute(now, which_axis, [(p, p ^ rr) for p in range(parts_n)])  27.8 us
    all_to_all x7, starting transfers between devices, window_work(): lax.all_to_all(send_channel, 'obs', split_axis=1, concat_axis=1, tiled=True)  26.2 us
    another operation x1, loops' own time, local(): lax.fori_loop(0, stream_count + section_count - 1, tick_step, initial)  26 us
    ppermute x21, starting transfers between devices, obtain_the_column(): lax.ppermute(now, which_axis, [(p, p ^ rr) for p in range(parts_n)])  21 us
  transfers between devices with their start and end apart: 42, of which 21 were waited for; matrix products, arithmetic and copies ran while one was open for 23% of the time, Pallas kernels for 0%

profile of v1, /device:TPU:1, one launch (start us, length us, event | category | flops | bytes accessed | tf_op | source)
XLA Modules:
  0.0 622.7 jit_solution(4866859668930999702)
XLA Ops:
  2.9 618.9 %while.38 = (s32[]{:T(128)}, f32[1,230,256]{2,1,0:T(8,128)S(1)}, f32[1,4,20,256]{3,1,2,0:T(4,128)S(1)}, f32[1,4,210,256]{3,1,2,0:T(4,128)S(1)}, s32[]{:T(128)}, ...) while((s32[]{:T(128)}, f32[1,230,256]{2,1,0:T(8,128)S(1)}, ...), condition=%wide.region_7.9_spmd.clone.clone, body=%wide.region_0.8_spmd.sunk.clone.clone.sunk | while | flops 57759520 | bytes 13853989 | solution.py:207
  7.5 6.4 %all-to-all-start.1 = ((f32[1,8,8]{2,0,1:T(1,128)}), f32[1,8,8]{2,0,1:T(1,128)S(1)}, u32[]{:S(2)}, u32[]{:S(2)}) async-start(f32[1,8,8]{2,0,1:T(1,128)} %bitcast.2462), calls=%async_computation.1 | async-start | bytes 8192 | tf_op jit(solution)/shard_map/while/body/eval_jaxpr/all_to_all | solution.py:168
  16.3 24.6 %all_gather.15 = f32[1,20,2048]{2,1,0:T(8,128)S(1)} all-gather(f32[1,20,256]{2,1,0:T(8,128)S(1)} %slice.5342), channel_id=1, replica_groups=mesh['section'=4,'obs'=8] {'obs'}, dimensions={2}, use_global_device_ids=true | all-gather | bytes 184320 | tf_op jit(solution)/shard_map/while/body/eval_jaxpr/all_gather | solution.py:152
  58.3 4.3 all-to-all-start
  74.5 14.9 %collective-permute-start.3 = (f32[1,230,256]{2,1,0:T(8,128)S(1)}, f32[1,230,256]{2,1,0:T(8,128)S(1)}, u32[]{:S(2)}, u32[]{:S(2)}) collective-permute-start(f32[1,230,256]{2,1,0:T(8,128)S(1)} %pad_maximum_fusion.2), channel_id=1, source_target_pairs={{0,8},{8,16},{16,24},{1,9},{9,17},{17,25},{2,10},{10,18},{18,26},{... | collective-permute-start | bytes 706568 | tf_op jit(solution)/shard_map/while/body/eval_jaxpr/ppermute | solution.py:22
  89.8 5.9 dynamic_update_slice.31
  106.1 25.2 %all_gather.15 = f32[1,20,2048]{2,1,0:T(8,128)S(1)} all-gather(f32[1,20,256]{2,1,0:T(8,128)S(1)} %slice.5342), channel_id=1, replica_groups=mesh['section'=4,'obs'=8] {'obs'}, dimensions={2}, use_global_device_ids=true | all-gather | bytes 184320 | tf_op jit(solution)/shard_map/while/body/eval_jaxpr/all_gather | solution.py:152
  164.6 12.5 %collective-permute-start.3 = (f32[1,230,256]{2,1,0:T(8,128)S(1)}, f32[1,230,256]{2,1,0:T(8,128)S(1)}, u32[]{:S(2)}, u32[]{:S(2)}) collective-permute-start(f32[1,230,256]{2,1,0:T(8,128)S(1)} %pad_maximum_fusion.2), channel_id=1, source_target_pairs={{0,8},{8,16},{16,24},{1,9},{9,17},{17,25},{2,10},{10,18},{18,26},{... | collective-permute-start | bytes 706568 | tf_op jit(solution)/shard_map/while/body/eval_jaxpr/ppermute | solution.py:22
  177.5 5.9 dynamic_update_slice.31
  193.8 24.8 %all_gather.15 = f32[1,20,2048]{2,1,0:T(8,128)S(1)} all-gather(f32[1,20,256]{2,1,0:T(8,128)S(1)} %slice.5342), channel_id=1, replica_groups=mesh['section'=4,'obs'=8] {'obs'}, dimensions={2}, use_global_device_ids=true | all-gather | bytes 184320 | tf_op jit(solution)/shard_map/while/body/eval_jaxpr/all_gather | solution.py:152
  252.2 12.6 %collective-permute-start.3 = (f32[1,230,256]{2,1,0:T(8,128)S(1)}, f32[1,230,256]{2,1,0:T(8,128)S(1)}, u32[]{:S(2)}, u32[]{:S(2)}) collective-permute-start(f32[1,230,256]{2,1,0:T(8,128)S(1)} %pad_maximum_fusion.2), channel_id=1, source_target_pairs={{0,8},{8,16},{16,24},{1,9},{9,17},{17,25},{2,10},{10,18},{18,26},{... | collective-permute-start | bytes 706568 | tf_op jit(solution)/shard_map/while/body/eval_jaxpr/ppermute | solution.py:22
  265.2 5.9 dynamic_update_slice.31
  281.4 24.8 %all_gather.15 = f32[1,20,2048]{2,1,0:T(8,128)S(1)} all-gather(f32[1,20,256]{2,1,0:T(8,128)S(1)} %slice.5342), channel_id=1, replica_groups=mesh['section'=4,'obs'=8] {'obs'}, dimensions={2}, use_global_device_ids=true | all-gather | bytes 184320 | tf_op jit(solution)/shard_map/while/body/eval_jaxpr/all_gather | solution.py:152
  340.1 12.4 %collective-permute-start.3 = (f32[1,230,256]{2,1,0:T(8,128)S(1)}, f32[1,230,256]{2,1,0:T(8,128)S(1)}, u32[]{:S(2)}, u32[]{:S(2)}) collective-permute-start(f32[1,230,256]{2,1,0:T(8,128)S(1)} %pad_maximum_fusion.2), channel_id=1, source_target_pairs={{0,8},{8,16},{16,24},{1,9},{9,17},{17,25},{2,10},{10,18},{18,26},{... | collective-permute-start | bytes 706568 | tf_op jit(solution)/shard_map/while/body/eval_jaxpr/ppermute | solution.py:22
  352.9 5.9 dynamic_update_slice.31
  369.1 24.9 %all_gather.15 = f32[1,20,2048]{2,1,0:T(8,128)S(1)} all-gather(f32[1,20,256]{2,1,0:T(8,128)S(1)} %slice.5342), channel_id=1, replica_groups=mesh['section'=4,'obs'=8] {'obs'}, dimensions={2}, use_global_device_ids=true | all-gather | bytes 184320 | tf_op jit(solution)/shard_map/while/body/eval_jaxpr/all_gather | solution.py:152
  427.5 12.7 %collective-permute-start.3 = (f32[1,230,256]{2,1,0:T(8,128)S(1)}, f32[1,230,256]{2,1,0:T(8,128)S(1)}, u32[]{:S(2)}, u32[]{:S(2)}) collective-permute-start(f32[1,230,256]{2,1,0:T(8,128)S(1)} %pad_maximum_fusion.2), channel_id=1, source_target_pairs={{0,8},{8,16},{16,24},{1,9},{9,17},{17,25},{2,10},{10,18},{18,26},{... | collective-permute-start | bytes 706568 | tf_op jit(solution)/shard_map/while/body/eval_jaxpr/ppermute | solution.py:22
  440.5 5.9 dynamic_update_slice.31
  456.8 24.8 %all_gather.15 = f32[1,20,2048]{2,1,0:T(8,128)S(1)} all-gather(f32[1,20,256]{2,1,0:T(8,128)S(1)} %slice.5342), channel_id=1, replica_groups=mesh['section'=4,'obs'=8] {'obs'}, dimensions={2}, use_global_device_ids=true | all-gather | bytes 184320 | tf_op jit(solution)/shard_map/while/body/eval_jaxpr/all_gather | solution.py:152
  515.3 12.5 %collective-permute-start.3 = (f32[1,230,256]{2,1,0:T(8,128)S(1)}, f32[1,230,256]{2,1,0:T(8,128)S(1)}, u32[]{:S(2)}, u32[]{:S(2)}) collective-permute-start(f32[1,230,256]{2,1,0:T(8,128)S(1)} %pad_maximum_fusion.2), channel_id=1, source_target_pairs={{0,8},{8,16},{16,24},{1,9},{9,17},{17,25},{2,10},{10,18},{18,26},{... | collective-permute-start | bytes 706568 | tf_op jit(solution)/shard_map/while/body/eval_jaxpr/ppermute | solution.py:22
  528.2 5.9 dynamic_update_slice.31
  544.5 24.5 %all_gather.15 = f32[1,20,2048]{2,1,0:T(8,128)S(1)} all-gather(f32[1,20,256]{2,1,0:T(8,128)S(1)} %slice.5342), channel_id=1, replica_groups=mesh['section'=4,'obs'=8] {'obs'}, dimensions={2}, use_global_device_ids=true | all-gather | bytes 184320 | tf_op jit(solution)/shard_map/while/body/eval_jaxpr/all_gather | solution.py:152
  603.1 12.4 %collective-permute-start.3 = (f32[1,230,256]{2,1,0:T(8,128)S(1)}, f32[1,230,256]{2,1,0:T(8,128)S(1)}, u32[]{:S(2)}, u32[]{:S(2)}) collective-permute-start(f32[1,230,256]{2,1,0:T(8,128)S(1)} %pad_maximum_fusion.2), channel_id=1, source_target_pairs={{0,8},{8,16},{16,24},{1,9},{9,17},{17,25},{2,10},{10,18},{18,26},{... | collective-permute-start | bytes 706568 | tf_op jit(solution)/shard_map/while/body/eval_jaxpr/ppermute | solution.py:22
  615.9 5.9 dynamic_update_slice.31
  (712 shorter events, 280.7 us)
Async XLA Ops:
  7.5 50.8 %all-to-all-start.1 = ((f32[1,8,8]{2,0,1:T(1,128)}), f32[1,8,8]{2,0,1:T(1,128)S(1)}, u32[]{:S(2)}, u32[]{:S(2)}) async-start(f32[1,8,8]{2,0,1:T(1,128)} %bitcast.2462), calls=%async_computation.1 | async-start | bytes 8192 | tf_op jit(solution)/shard_map/while/body/eval_jaxpr/all_to_all | solution.py:168
  58.3 10.0 %all-to-all-start = ((f32[1,8,8,230]{3,2,0,1:T(8,128)}), f32[1,8,8,230]{3,2,0,1:T(8,128)S(1)}, u32[]{:S(2)}, u32[]{:S(2)}) async-start(f32[1,8,8,230]{3,2,0,1:T(8,128)} %convolution_bitcast_fusion.4), calls=%async_computation | async-start | bytes 131072 | tf_op jit(solution)/shard_map/while/body/eval_jaxpr/all_to_all | solution.py:167
  74.5 21.2 %collective-permute-start.3 = (f32[1,230,256]{2,1,0:T(8,128)S(1)}, f32[1,230,256]{2,1,0:T(8,128)S(1)}, u32[]{:S(2)}, u32[]{:S(2)}) collective-permute-start(f32[1,230,256]{2,1,0:T(8,128)S(1)} %pad_maximum_fusion.2), channel_id=1, source_target_pairs={{0,8},{8,16},{16,24},{1,9},{9,17},{17,25},{2,10},{10,18},{18,26},{... | collective-permute-start | bytes 706568 | tf_op jit(solution)/shard_map/while/body/eval_jaxpr/ppermute | solution.py:22
  100.3 48.0 %all-to-all-start.1 = ((f32[1,8,8]{2,0,1:T(1,128)}), f32[1,8,8]{2,0,1:T(1,128)S(1)}, u32[]{:S(2)}, u32[]{:S(2)}) async-start(f32[1,8,8]{2,0,1:T(1,128)} %bitcast.2462), calls=%async_computation.1 | async-start | bytes 8192 | tf_op jit(solution)/shard_map/while/body/eval_jaxpr/all_to_all | solution.py:168
  148.4 10.0 %all-to-all-start = ((f32[1,8,8,230]{3,2,0,1:T(8,128)}), f32[1,8,8,230]{3,2,0,1:T(8,128)S(1)}, u32[]{:S(2)}, u32[]{:S(2)}) async-start(f32[1,8,8,230]{3,2,0,1:T(8,128)} %convolution_bitcast_fusion.4), calls=%async_computation | async-start | bytes 131072 | tf_op jit(solution)/shard_map/while/body/eval_jaxpr/all_to_all | solution.py:167
  164.6 18.8 %collective-permute-start.3 = (f32[1,230,256]{2,1,0:T(8,128)S(1)}, f32[1,230,256]{2,1,0:T(8,128)S(1)}, u32[]{:S(2)}, u32[]{:S(2)}) collective-permute-start(f32[1,230,256]{2,1,0:T(8,128)S(1)} %pad_maximum_fusion.2), channel_id=1, source_target_pairs={{0,8},{8,16},{16,24},{1,9},{9,17},{17,25},{2,10},{10,18},{18,26},{... | collective-permute-start | bytes 706568 | tf_op jit(solution)/shard_map/while/body/eval_jaxpr/ppermute | solution.py:22
  188.0 48.0 %all-to-all-start.1 = ((f32[1,8,8]{2,0,1:T(1,128)}), f32[1,8,8]{2,0,1:T(1,128)S(1)}, u32[]{:S(2)}, u32[]{:S(2)}) async-start(f32[1,8,8]{2,0,1:T(1,128)} %bitcast.2462), calls=%async_computation.1 | async-start | bytes 8192 | tf_op jit(solution)/shard_map/while/body/eval_jaxpr/all_to_all | solution.py:168
  236.0 10.0 %all-to-all-start = ((f32[1,8,8,230]{3,2,0,1:T(8,128)}), f32[1,8,8,230]{3,2,0,1:T(8,128)S(1)}, u32[]{:S(2)}, u32[]{:S(2)}) async-start(f32[1,8,8,230]{3,2,0,1:T(8,128)} %convolution_bitcast_fusion.4), calls=%async_computation | async-start | bytes 131072 | tf_op jit(solution)/shard_map/while/body/eval_jaxpr/all_to_all | solution.py:167
  252.2 18.9 %collective-permute-start.3 = (f32[1,230,256]{2,1,0:T(8,128)S(1)}, f32[1,230,256]{2,1,0:T(8,128)S(1)}, u32[]{:S(2)}, u32[]{:S(2)}) collective-permute-start(f32[1,230,256]{2,1,0:T(8,128)S(1)} %pad_maximum_fusion.2), channel_id=1, source_target_pairs={{0,8},{8,16},{16,24},{1,9},{9,17},{17,25},{2,10},{10,18},{18,26},{... | collective-permute-start | bytes 706568 | tf_op jit(solution)/shard_map/while/body/eval_jaxpr/ppermute | solution.py:22
  275.7 48.2 %all-to-all-start.1 = ((f32[1,8,8]{2,0,1:T(1,128)}), f32[1,8,8]{2,0,1:T(1,128)S(1)}, u32[]{:S(2)}, u32[]{:S(2)}) async-start(f32[1,8,8]{2,0,1:T(1,128)} %bitcast.2462), calls=%async_computation.1 | async-start | bytes 8192 | tf_op jit(solution)/shard_map/while/body/eval_jaxpr/all_to_all | solution.py:168
  311.4 4.2 collective-permute-start
  323.9 10.0 %all-to-all-start = ((f32[1,8,8,230]{3,2,0,1:T(8,128)}), f32[1,8,8,230]{3,2,0,1:T(8,128)S(1)}, u32[]{:S(2)}, u32[]{:S(2)}) async-start(f32[1,8,8,230]{3,2,0,1:T(8,128)} %convolution_bitcast_fusion.4), calls=%async_computation | async-start | bytes 131072 | tf_op jit(solution)/shard_map/while/body/eval_jaxpr/all_to_all | solution.py:167
  340.1 18.7 %collective-permute-start.3 = (f32[1,230,256]{2,1,0:T(8,128)S(1)}, f32[1,230,256]{2,1,0:T(8,128)S(1)}, u32[]{:S(2)}, u32[]{:S(2)}) collective-permute-start(f32[1,230,256]{2,1,0:T(8,128)S(1)} %pad_maximum_fusion.2), channel_id=1, source_target_pairs={{0,8},{8,16},{16,24},{1,9},{9,17},{17,25},{2,10},{10,18},{18,26},{... | collective-permute-start | bytes 706568 | tf_op jit(solution)/shard_map/while/body/eval_jaxpr/ppermute | solution.py:22
  363.4 48.2 %all-to-all-start.1 = ((f32[1,8,8]{2,0,1:T(1,128)}), f32[1,8,8]{2,0,1:T(1,128)S(1)}, u32[]{:S(2)}, u32[]{:S(2)}) async-start(f32[1,8,8]{2,0,1:T(1,128)} %bitcast.2462), calls=%async_computation.1 | async-start | bytes 8192 | tf_op jit(solution)/shard_map/while/body/eval_jaxpr/all_to_all | solution.py:168
  411.6 9.7 %all-to-all-start = ((f32[1,8,8,230]{3,2,0,1:T(8,128)}), f32[1,8,8,230]{3,2,0,1:T(8,128)S(1)}, u32[]{:S(2)}, u32[]{:S(2)}) async-start(f32[1,8,8,230]{3,2,0,1:T(8,128)} %convolution_bitcast_fusion.4), calls=%async_computation | async-start | bytes 131072 | tf_op jit(solution)/shard_map/while/body/eval_jaxpr/all_to_all | solution.py:167
  427.5 19.0 %collective-permute-start.3 = (f32[1,230,256]{2,1,0:T(8,128)S(1)}, f32[1,230,256]{2,1,0:T(8,128)S(1)}, u32[]{:S(2)}, u32[]{:S(2)}) collective-permute-start(f32[1,230,256]{2,1,0:T(8,128)S(1)} %pad_maximum_fusion.2), channel_id=1, source_target_pairs={{0,8},{8,16},{16,24},{1,9},{9,17},{17,25},{2,10},{10,18},{18,26},{... | collective-permute-start | bytes 706568 | tf_op jit(solution)/shard_map/while/body/eval_jaxpr/ppermute | solution.py:22
  451.1 48.1 %all-to-all-start.1 = ((f32[1,8,8]{2,0,1:T(1,128)}), f32[1,8,8]{2,0,1:T(1,128)S(1)}, u32[]{:S(2)}, u32[]{:S(2)}) async-start(f32[1,8,8]{2,0,1:T(1,128)} %bitcast.2462), calls=%async_computation.1 | async-start | bytes 8192 | tf_op jit(solution)/shard_map/while/body/eval_jaxpr/all_to_all | solution.py:168
  486.7 4.1 collective-permute-start
  499.1 10.0 %all-to-all-start = ((f32[1,8,8,230]{3,2,0,1:T(8,128)}), f32[1,8,8,230]{3,2,0,1:T(8,128)S(1)}, u32[]{:S(2)}, u32[]{:S(2)}) async-start(f32[1,8,8,230]{3,2,0,1:T(8,128)} %convolution_bitcast_fusion.4), calls=%async_computation | async-start | bytes 131072 | tf_op jit(solution)/shard_map/while/body/eval_jaxpr/all_to_all | solution.py:167
  515.3 18.8 %collective-permute-start.3 = (f32[1,230,256]{2,1,0:T(8,128)S(1)}, f32[1,230,256]{2,1,0:T(8,128)S(1)}, u32[]{:S(2)}, u32[]{:S(2)}) collective-permute-start(f32[1,230,256]{2,1,0:T(8,128)S(1)} %pad_maximum_fusion.2), channel_id=1, source_target_pairs={{0,8},{8,16},{16,24},{1,9},{9,17},{17,25},{2,10},{10,18},{18,26},{... | collective-permute-start | bytes 706568 | tf_op jit(solution)/shard_map/while/body/eval_jaxpr/ppermute | solution.py:22
  538.7 48.2 %all-to-all-start.1 = ((f32[1,8,8]{2,0,1:T(1,128)}), f32[1,8,8]{2,0,1:T(1,128)S(1)}, u32[]{:S(2)}, u32[]{:S(2)}) async-start(f32[1,8,8]{2,0,1:T(1,128)} %bitcast.2462), calls=%async_computation.1 | async-start | bytes 8192 | tf_op jit(solution)/shard_map/while/body/eval_jaxpr/all_to_all | solution.py:168
  574.0 4.5 collective-permute-start
  586.9 10.0 %all-to-all-start = ((f32[1,8,8,230]{3,2,0,1:T(8,128)}), f32[1,8,8,230]{3,2,0,1:T(8,128)S(1)}, u32[]{:S(2)}, u32[]{:S(2)}) async-start(f32[1,8,8,230]{3,2,0,1:T(8,128)} %convolution_bitcast_fusion.4), calls=%async_computation | async-start | bytes 131072 | tf_op jit(solution)/shard_map/while/body/eval_jaxpr/all_to_all | solution.py:167
  603.1 18.7 %collective-permute-start.3 = (f32[1,230,256]{2,1,0:T(8,128)S(1)}, f32[1,230,256]{2,1,0:T(8,128)S(1)}, u32[]{:S(2)}, u32[]{:S(2)}) collective-permute-start(f32[1,230,256]{2,1,0:T(8,128)S(1)} %pad_maximum_fusion.2), channel_id=1, source_target_pairs={{0,8},{8,16},{16,24},{1,9},{9,17},{17,25},{2,10},{10,18},{18,26},{... | collective-permute-start | bytes 706568 | tf_op jit(solution)/shard_map/while/body/eval_jaxpr/ppermute | solution.py:22
  (44 other events, 73.9 us)
